TPU v7x, 256 devices: a whole 4x4x8 slice. The times are simulated.
256 devices in a mesh: context: 32 (over z, x_lo, core), tensor: 8 (over x_hi, y).
Axes of the slice: x: 4 (x_hi: 2, x_lo: 2; x = x_hi * 2 + x_lo), y: 4, z: 8, core: 2. Of those that a mesh axis runs over, the one named last changes fastest.
Arguments:
- activations: bfloat16 [6144, 5120], P(('context', 'tensor')), may hold values from -6 to 6
- queries: bfloat16 [6144, 5120], P('context', 'tensor'), may hold values from -44 to 44
- key_weight: bfloat16 [5120, 1024], P(None, 'tensor'), may hold values from -0.5 to 1.1
- value_projection_weight: bfloat16 [5120, 1024], P(None, 'tensor'), may hold values from -0.078125 to 0.078125
- output_gradient: bfloat16 [6144, 5120], P('context', 'tensor'), may hold values from -6 to 6
- span_order: int32 [64], replicated, may hold values from 0 to 63, as said below
- doc_ids: int32 [6144], replicated, may hold values from 0 to 4, as said below
Outputs:
- attended: bfloat16 [6144, 5120], P('context', 'tensor')
- grad_queries: bfloat16 [6144, 5120], P('context', 'tensor')
- grad_inputs: bfloat16 [6144, 5120], P(('context', 'tensor'))
- grad_key_weight: float32 [5120, 1024], P('context', 'tensor')
- grad_value_weight: float32 [5120, 1024], P('context', 'tensor')
Inputs may be any that keep to these rules, and one draw needn't show every extreme that they name: `span_order`: each number once. `doc_ids`: taken in order of positions, the document numbers never fall; one document holds exactly 3072 positions and none holds more.
All inputs are finite; a program needn't handle non-finite values.
Results may differ from a plain program's by a relative error of at most 0.02.
Values may be sent and summed in bfloat16 or wider, within the bound.
No kernel may reach another device: no remote copies, remote signals or barrier semaphores. Data moves between devices by JAX's collectives and lax.ppermute only.
A program may use at most 192 MiB of HBM per device.

v0:
```python
import math

import jax
import jax.numpy as jnp
from jax import lax
from jax.sharding import PartitionSpec as P

HEAD_SIZE = 128
SPAN = 96


def on_device(
    activations, queries, key_weight, value_projection_weight, output_gradient, span_order, doc_ids
):
    local_rows = lax.all_gather(activations, "tensor", axis=0, tiled=True)
    shard_len = local_rows.shape[0]
    seq_len = doc_ids.shape[0]
    head_dim = HEAD_SIZE
    kv_width = key_weight.shape[1]
    kv_heads = kv_width // head_dim
    heads_per_group = queries.shape[1] // kv_width
    inv_root = 1.0 / math.sqrt(head_dim)
    key_local = jnp.dot(local_rows, key_weight, preferred_element_type=jnp.float32).astype(
        jnp.bfloat16
    )
    value_local = jnp.dot(
        local_rows, value_projection_weight, preferred_element_type=jnp.float32
    ).astype(jnp.bfloat16)
    row_ids = jnp.arange(seq_len, dtype=jnp.int32)
    span_match = (row_ids // SPAN)[:, None] == jnp.arange(span_order.shape[0], dtype=jnp.int32)[
        None, :
    ]
    all_pos = jnp.sum(jnp.where(span_match, span_order[None, :], 0), axis=1) * SPAN + row_ids % SPAN
    first_row = lax.axis_index("context") * shard_len
    query_pos = lax.dynamic_slice_in_dim(all_pos, first_row, shard_len)
    query_doc = lax.dynamic_slice_in_dim(doc_ids, first_row, shard_len)
    query_heads = queries.reshape(shard_len, kv_heads, heads_per_group, head_dim)
    grad_heads = output_gradient.reshape(shard_len, kv_heads, heads_per_group, head_dim)

    def visible():
        pair_mask = (query_doc[:, None] == doc_ids[None, :]) & (
            all_pos[None, :] <= query_pos[:, None]
        )
        return pair_mask[:, None, None, :]

    def scores_of(key_heads_split):
        return (
            jnp.einsum(
                "sgjd,ngd->sgjn", query_heads, key_heads_split, preferred_element_type=jnp.float32
            )
            * inv_root
        )

    stats_shape = (shard_len, kv_heads, heads_per_group)
    run_max = jnp.full(stats_shape, -1e30, jnp.float32)
    key_piece = lax.all_gather(key_local, "context", axis=0, tiled=True)
    value_piece = lax.all_gather(value_local, "context", axis=0, tiled=True)
    piece_len = key_piece.shape[0]
    pair_mask = visible()
    scores = scores_of(key_piece.reshape(piece_len, kv_heads, head_dim))
    new_max = jnp.maximum(run_max, jnp.max(jnp.where(pair_mask, scores, -1e30), axis=3))
    weights = jnp.where(pair_mask, jnp.exp(scores - new_max[..., None]), 0.0)
    value_heads_split = value_piece.reshape(piece_len, kv_heads, head_dim)
    summed = jnp.einsum(
        "sgjn,ngd->sgjd",
        weights.astype(jnp.bfloat16),
        value_heads_split,
        preferred_element_type=jnp.float32,
    )
    final_sum = jnp.sum(weights, axis=3)
    attended_low = (summed / final_sum[..., None]).astype(jnp.bfloat16)
    log_totals = new_max + jnp.log(final_sum)
    row_delta = jnp.sum(grad_heads.astype(jnp.float32) * attended_low.astype(jnp.float32), axis=3)
    key_piece = lax.all_gather(key_local, "context", axis=0, tiled=True)
    value_piece = lax.all_gather(value_local, "context", axis=0, tiled=True)
    piece_len = key_piece.shape[0]
    score_piece_len = key_piece.shape[0]
    pair_mask = visible()
    key_heads_split = key_piece.reshape(score_piece_len, kv_heads, head_dim)
    value_heads_split = value_piece.reshape(score_piece_len, kv_heads, head_dim)
    scores = scores_of(key_heads_split)
    probs = jnp.where(pair_mask, jnp.exp(scores - log_totals[..., None]), 0.0)
    grad_probs = jnp.einsum(
        "sgjd,ngd->sgjn", grad_heads, value_heads_split, preferred_element_type=jnp.float32
    )
    grad_scores = (probs * (grad_probs - row_delta[..., None]) * inv_root).astype(jnp.bfloat16)
    probs, grad_scores, key_heads_split = (probs, grad_scores, key_heads_split)
    grad_v_part = jnp.einsum(
        "sgjn,sgjd->ngd", probs.astype(jnp.bfloat16), grad_heads, preferred_element_type=jnp.float32
    )
    grad_q = jnp.einsum(
        "sgjn,ngd->sgjd", grad_scores, key_heads_split, preferred_element_type=jnp.float32
    )
    grad_k_part = jnp.einsum(
        "sgjn,sgjd->ngd", grad_scores, query_heads, preferred_element_type=jnp.float32
    )
    grad_k_buf = grad_k_part.reshape(piece_len, kv_width)
    grad_v_buf = grad_v_part.reshape(piece_len, kv_width)
    grad_q, grad_k_buf, grad_v_buf = (grad_q, grad_k_buf, grad_v_buf)
    grad_k_own, grad_v_own = (
        lax.psum_scatter(
            grad_k_buf.astype(jnp.bfloat16), "context", scatter_dimension=0, tiled=True
        ).astype(jnp.float32),
        lax.psum_scatter(
            grad_v_buf.astype(jnp.bfloat16), "context", scatter_dimension=0, tiled=True
        ).astype(jnp.float32),
    )
    grad_k_low = grad_k_own.astype(jnp.bfloat16)
    grad_v_low = grad_v_own.astype(jnp.bfloat16)
    grad_inputs = lax.psum_scatter(
        (
            jnp.dot(grad_k_low, key_weight.T, preferred_element_type=jnp.float32)
            + jnp.dot(grad_v_low, value_projection_weight.T, preferred_element_type=jnp.float32)
        ).astype(jnp.bfloat16),
        "tensor",
        scatter_dimension=0,
        tiled=True,
    )
    grad_kv = jnp.concatenate([grad_k_low, grad_v_low], axis=1)
    partial_grads = lax.dot_general(
        local_rows, grad_kv, (((0,), (0,)), ((), ())), preferred_element_type=jnp.float32
    )
    weight_grads = lax.psum_scatter(
        partial_grads.astype(jnp.bfloat16), "context", scatter_dimension=0, tiled=True
    ).astype(jnp.float32)
    attended = attended_low.reshape(shard_len, heads_per_group * kv_width)
    grad_queries = grad_q.astype(jnp.bfloat16).reshape(shard_len, heads_per_group * kv_width)
    return (
        attended,
        grad_queries,
        grad_inputs,
        weight_grads[:, :kv_width],
        weight_grads[:, kv_width:],
    )


def solution(mesh):
    return jax.shard_map(
        on_device,
        mesh=mesh,
        in_specs=(
            P(("context", "tensor"), None),
            P("context", "tensor"),
            P(None, "tensor"),
            P(None, "tensor"),
            P("context", "tensor"),
            P(),
            P(),
        ),
        out_specs=(
            P("context", "tensor"),
            P("context", "tensor"),
            P(("context", "tensor"), None),
            P("context", "tensor"),
            P("context", "tensor"),
        ),
        check_vma=False,
    )
```

profile of v0, /device:TPU:32, one launch (start us, length us, event | category | flops | bytes accessed | tf_op | source)
XLA Modules:
  0.0 701.8 jit_solution(13686100925459275635)
XLA Ops:
  7.2 0.0 copy-start
  7.2 0.0 copy-start.5
  7.2 0.0 copy-start.9
  7.2 0.0 copy-start.8
  7.2 0.0 all-gather.4.cloned.1.call-start
  7.3 0.7 all-gather.4.cloned.1.call-update
  7.9 0.0 all-gather.8.cloned.1.call-start
  8.0 62.8 %all-gather.4.cloned.1.call-done = bf16[192,5120]{1,0:T(8,128)(2,1)} async-done(((bf16[24,5120]{1,0:T(8,128)(2,1)}), bf16[192,5120]{1,0:T(8,128)(2,1)}) %all-gather.4.cloned.1.call-update) | async-done | bytes 1966096 | tf_op jit(solution)/shard_map/all_gather | solution.py:15
  70.8 0.0 copy-done
  70.8 0.0 copy-start.1
  70.8 3.0 convolution_convert_fusion.1
  73.8 0.0 all-gather.8.cloned.1.call-update
  73.8 0.0 all-gather.6.cloned.1.call-start
  73.9 2.0 copy.51
  75.8 0.0 copy-done.5
  75.8 0.9 copy.49
  76.7 2.1 copy.52
  78.9 0.0 copy-done.9
  78.9 0.3 select_reduce_fusion
  79.2 0.1 dynamic_slice.7
  79.3 0.0 copy-done.8
  79.3 0.1 dynamic_slice.6
  79.4 1.8 copy.46
  81.2 2.0 compare_and_fusion
  83.2 0.0 copy-done.1
  83.2 2.6 convolution_convert_fusion.2
  85.9 0.0 all-gather.6.cloned.1.call-update
  85.9 0.0 reduce-scatter.7.cloned.1.call-start
  85.9 49.3 %all-gather.8.cloned.1.call-done = bf16[6144,128]{1,0:T(8,128)(2,1)} async-done(((bf16[192,128]{1,0:T(8,128)(2,1)}), bf16[6144,128]{1,0:T(8,128)(2,1)}) %all-gather.8.cloned.1.call-update) | async-done | bytes 1572880 | tf_op jit(solution)/shard_map/all_gather | solution.py:56
  135.3 11.6 %fusion.2 = (f32[192,5]{0,1:T(8,128)S(1)}, f32[6144,192,5]{0,1,2:T(8,128)}) fusion(pred[192,6144]{1,0:T(8,128)(4,1)} %compare_and_fusion, bf16[192,5,128]{0,2,1:T(8,128)(2,1)} %bitcast.161, bf16[6144,128]{1,0:T(8,128)(2,1)} %all-gather.8.cloned.1.call-done), kind=kOutput, calls=%fused_computation.7 | convolution fusion | flops 1527643136 | bytes 26595072 | tf_op jit(solution)/shard_map/sgjd,ngd->sgjn/dot_general | solution.py:48
  146.8 0.0 copy-done.3
  146.9 11.4 %fusion.8 = f32[192,5]{0,1:T(8,128)S(1)} fusion(f32[6144,192,5]{0,1,2:T(8,128)} %get-tuple-element.28, f32[192,5]{0,1:T(8,128)S(1)} %broadcast_maximum_fusion, pred[192,6144]{1,0:T(8,128)(4,1)S(1)} %copy-done.3), kind=kLoop, calls=%fused_computation.13 | loop fusion | flops 23592000 | bytes 24780288 | tf_op jit(solution)/shard_map/reduce_sum | solution.py:70
  158.3 43.2 %all-gather.6.cloned.1.call-done = bf16[6144,128]{1,0:T(8,128)(2,1)} async-done(((bf16[192,128]{1,0:T(8,128)(2,1)}), bf16[6144,128]{1,0:T(8,128)(2,1)}) %all-gather.6.cloned.1.call-update) | async-done | bytes 1572880 | tf_op jit(solution)/shard_map/all_gather | solution.py:57
  201.5 13.0 %multiply_reduce_fusion = (f32[192,5]{0,1:T(8,128)S(1)}, bf16[192,1,5,128]{3,0,2,1:T(8,128)(2,1)S(1)}) fusion(f32[192,1,5,128]{3,0,2,1:T(8,128)} %copy.52, f32[192,5]{0,1:T(8,128)S(1)} %fusion.8, f32[6144,192,5]{0,1,2:T(8,128)} %get-tuple-element.28, f32[192,5]{0,1:T(8,128)S(1)} %broadcast_maximum_fusion, pred[192,6144]{1,0:T(8,128)(4,1)} %compare_and_fusion, ...), kind=kOutput, calls=%fused_computation.49 | convolution fusion | flops 1534155776 | bytes 27094272 | tf_op jit(solution)/shard_map/sgjn,ngd->sgjd/dot_general | solution.py:64
  214.5 19.3 %fusion.1 = bf16[192,1,5,6144]{3,0,2,1:T(8,128)(2,1)} fusion(f32[6144,192,5]{0,1,2:T(8,128)} %get-tuple-element.28, bf16[192,5,128]{0,2,1:T(8,128)(2,1)} %bitcast.159, f32[192,5]{0,1:T(8,128)S(1)} %get-tuple-element.29, f32[192,5]{0,1:T(8,128)S(1)} %log_add_fusion, pred[192,6144]{1,0:T(8,128)(4,1)} %compare_and_fusion, ...), kind=kOutput, calls=%fused_computation.2 | convolution fusion | flops 1551237120 | bytes 38395392 | tf_op jit(solution)/shard_map/sgjd,ngd->sgjn/dot_general | solution.py:83
  233.8 9.9 %fusion.31 = bf16[6144,128]{1,0:T(8,128)(2,1)} fusion(bf16[192,5,128]{0,2,1:T(8,128)(2,1)} %bitcast.162, bf16[192,1,5,6144]{3,0,2,1:T(8,128)(2,1)} %fusion.1), kind=kOutput, calls=%fused_computation.28 | convolution fusion | flops 1510735872 | bytes 13615104 | tf_op jit(solution)/shard_map/sgjn,sgjd->ngd/dot_general | solution.py:94
  243.7 0.0 reduce-scatter.7.cloned.1.call-update
  243.7 0.0 reduce-scatter.9.cloned.1.call-start
  243.8 12.6 %fusion.28 = bf16[6144,128]{1,0:T(8,128)(2,1)} fusion(bf16[192,5,128]{0,2,1:T(8,128)(2,1)} %bitcast.160, f32[6144,192,5]{0,1,2:T(8,128)} %get-tuple-element.28, f32[192,5]{0,1:T(8,128)S(1)} %log_add_fusion, pred[192,6144]{1,0:T(8,128)(4,1)} %compare_and_fusion), kind=kOutput, calls=%fused_computation.27 | convolution fusion | flops 1534328832 | bytes 26595072 | tf_op jit(solution)/shard_map/sgjn,sgjd->ngd/dot_general | solution.py:88
  256.4 0.0 reduce-scatter.9.cloned.1.call-update
  256.4 0.0 reduce-scatter.13.cloned.1.call-start
  256.4 100.9 %reduce-scatter.7.cloned.1.call-done = bf16[192,128]{1,0:T(8,128)(2,1)} async-done(((bf16[6144,128]{1,0:T(8,128)(2,1)}), bf16[192,128]{1,0:T(8,128)(2,1)}) %reduce-scatter.7.cloned.1.call-update) | async-done | bytes 49168 | tf_op jit(solution)/shard_map/reduce_scatter | solution.py:101
  357.4 120.2 %reduce-scatter.9.cloned.1.call-done = bf16[192,128]{1,0:T(8,128)(2,1)} async-done(((bf16[6144,128]{1,0:T(8,128)(2,1)}), bf16[192,128]{1,0:T(8,128)(2,1)}) %reduce-scatter.9.cloned.1.call-update) | async-done | bytes 49168 | tf_op jit(solution)/shard_map/reduce_scatter | solution.py:104
  477.6 3.2 fusion.35
  480.8 4.4 copy.64
  485.2 0.0 reduce-scatter.13.cloned.1.call-update
  485.3 0.0 reduce-scatter.11.cloned.1.call-start
  485.3 0.0 copy-done.6
  485.3 0.7 fusion.88
  486.0 0.6 copy-done.2
  486.5 0.0 copy-done.7
  486.5 2.0 fusion.34
  488.5 0.0 reduce-scatter.11.cloned.1.call-update
  488.6 0.2 copy.48
  488.8 0.9 copy.56
  489.6 0.4 copy-done.4
  490.0 6.1 fusion.51
  496.2 0.2 copy.53
  496.3 0.9 copy.57
  497.2 107.8 %reduce-scatter.13.cloned.1.call-done = bf16[160,256]{1,0:T(8,128)(2,1)} async-done(((bf16[5120,256]{1,0:T(8,128)(2,1)}), bf16[160,256]{1,0:T(8,128)(2,1)}) %reduce-scatter.13.cloned.1.call-update) | async-done | bytes 81936
  605.0 1.0 copy.65
  606.1 0.7 copy.58
  606.8 0.7 copy.59
  607.5 87.4 %reduce-scatter.11.cloned.1.call-done = bf16[24,5120]{1,0:T(8,128)(2,1)} async-done(((bf16[192,5120]{1,0:T(8,128)(2,1)}), bf16[24,5120]{1,0:T(8,128)(2,1)}) %reduce-scatter.11.cloned.1.call-update) | async-done | bytes 245776 | tf_op jit(solution)/shard_map/reduce_scatter | solution.py:110
  (10 shorter events, 0.1 us)
Async XLA Ops:
  7.2 63.6 %copy-start = (bf16[5120,128]{1,0:T(8,128)(2,1)S(1)}, bf16[5120,128]{1,0:T(8,128)(2,1)}, u32[]{:S(2)}) copy-start(bf16[5120,128]{1,0:T(8,128)(2,1)} %param.9) | copy-start | bytes 3932164
  7.2 68.6 %copy-start.5 = (bf16[192,640]{1,0:T(8,128)(2,1)S(1)}, bf16[192,640]{1,0:T(8,128)(2,1)}, u32[]{:S(2)}) copy-start(bf16[192,640]{1,0:T(8,128)(2,1)} %param.11) | copy-start | bytes 737284
  7.2 71.7 %copy-start.9 = (s32[64]{0:T(128)S(1)}, s32[64]{0:T(128)}, u32[]{:S(2)}) copy-start(s32[64]{0:T(128)} %param.12) | copy-start | bytes 772
  7.2 72.1 %copy-start.8 = (s32[6144]{0:T(1024)S(1)}, s32[6144]{0:T(1024)}, u32[]{:S(2)}) copy-start(s32[6144]{0:T(1024)} %param.13) | copy-start | bytes 73732
  7.2 63.6 %all-gather.4.cloned.1.call-start = ((), (), s32[]{:S(2)}) async-start(), calls=%async_computation.4 | async-start | bytes 2211840 | tf_op jit(solution)/shard_map/all_gather | solution.py:15
  7.9 127.3 %all-gather.8.cloned.1.call-start = ((), (), s32[]{:S(2)}) async-start(), calls=%async_computation.6 | async-start | bytes 1622016 | tf_op jit(solution)/shard_map/all_gather | solution.py:56
  70.8 12.4 %copy-start.1 = (bf16[192,5120]{1,0:T(8,128)(2,1)S(1)}, bf16[192,5120]{1,0:T(8,128)(2,1)}, u32[]{:S(2)}) copy-start(bf16[192,5120]{1,0:T(8,128)(2,1)} %all-gather.4.cloned.1.call-done) | copy-start | bytes 5898244
  73.8 127.7 %all-gather.6.cloned.1.call-start = ((), (), s32[]{:S(2)}) async-start(), calls=%async_computation.5 | async-start | bytes 1622016 | tf_op jit(solution)/shard_map/all_gather | solution.py:57
  85.9 271.5 %reduce-scatter.7.cloned.1.call-start = ((), (), s32[]{:S(2)}) async-start(), calls=%async_computation.7 | async-start | bytes 1622016 | tf_op jit(solution)/shard_map/reduce_scatter | solution.py:101
  135.3 11.6 %copy-start.3 = (pred[192,6144]{1,0:T(8,128)(4,1)S(1)}, pred[192,6144]{1,0:T(8,128)(4,1)}, u32[]{:S(2)}) copy-start(pred[192,6144]{1,0:T(8,128)(4,1)} %compare_and_fusion) | copy-start | bytes 3538948
  243.7 233.9 %reduce-scatter.9.cloned.1.call-start = ((), (), s32[]{:S(2)}) async-start(), calls=%async_computation.8 | async-start | bytes 1622016 | tf_op jit(solution)/shard_map/reduce_scatter | solution.py:104
  256.4 348.7 %reduce-scatter.13.cloned.1.call-start = ((), (), s32[]{:S(2)}) async-start(), calls=%async_computation.10 | async-start | bytes 2703360
  480.8 4.5 copy-start.6
  485.2 1.3 copy-start.2
  485.2 1.3 copy-start.7
  485.3 209.7 %reduce-scatter.11.cloned.1.call-start = ((), (), s32[]{:S(2)}) async-start(), calls=%async_computation.9 | async-start | bytes 2211840 | tf_op jit(solution)/shard_map/reduce_scatter | solution.py:110
  488.5 1.5 copy-start.4
Sparse Core Ops, SparseCore 0:
  10.6 60.1 all-gather.3
  73.9 61.2 all-gather.7
  137.7 63.7 all-gather.5
  243.9 113.4 reduce-scatter.6
  359.7 117.8 reduce-scatter.8
  485.4 119.6 reduce-scatter.12
  609.6 85.2 reduce-scatter.10
where the time goes:
time: 702 us
  waiting for transfers between devices  573 us (82%)
  matrix products  83.9 us (12%)
  local copies, waits for them, and re-layouts  16.9 us (2%)
  between operations  14.3 us (2%)
  other arithmetic  13.8 us (2%)
    reduce_scatter x1, waiting for transfers between devices, on_device(): lax.psum_scatter(grad_v_buf.astype(jnp.bfloat16), 'context', scatter_dime...  120 us
    unnamed x8, waiting for transfers between devices  109 us
    reduce_scatter x1, waiting for transfers between devices, on_device(): lax.psum_scatter(grad_k_buf.astype(jnp.bfloat16), 'context', scatter_dime...  101 us
    reduce_scatter x1, waiting for transfers between devices, on_device(): lax.psum_scatter((jnp.dot(grad_k_low, key_weight.T, preferred_element_typ...  87.4 us
    all_gather x1, waiting for transfers between devices, on_device(): local_rows = lax.all_gather(activations, 'tensor', axis=0, tiled=True)  62.8 us
    all_gather x1, waiting for transfers between devices, on_device(): key_piece = lax.all_gather(key_local, 'context', axis=0, tiled=True)  49.3 us
    all_gather x1, waiting for transfers between devices, on_device(): value_piece = lax.all_gather(value_local, 'context', axis=0, tiled=True)  43.2 us
    dot_general x1, matrix products, on_device(): jnp.einsum('sgjd,ngd->sgjn', grad_heads, value_heads_split, preferred_ele...  19.3 us
  transfers between devices with their start and end apart: 7, of which 7 were waited for; matrix products, arithmetic and copies ran while one was open for 9% of the time, Pallas kernels for 0%

commit v1 on v0

v1 whole, which is shorter than its diff:
```python
import functools
import math

import jax
import jax.numpy as jnp
from jax import lax
from jax.experimental import pallas as pl
from jax.experimental.pallas import tpu as pltpu
from jax.sharding import Mesh, PartitionSpec as P


HEAD = 128
SPAN = 96
GROUP = 4
BLOCK = GROUP * SPAN
CTX = ("z", "xl", "c")
TEN = ("xh", "y")
MASKED = -1e30


def brought(n_z):
    far = n_z // 2
    steps = [0] + [s * k for k in range(1, far) for s in (1, -1)]
    return [(k, side) for k in steps for side in (0, 1)] + [(far, 0), (far, 1)]


def attention_kernel(n_near, table_ref, limit_ref, q_ref, g_ref, *refs):
    blocks, refs = refs[: 2 * n_near], refs[2 * n_near :]
    att_ref, gq_ref = refs[:2]
    outs, (kv_s, acc_s, s_s, qs, gs) = refs[2:10], refs[10:]
    halves = q_ref.shape[0] // SPAN
    n_slots = outs[0].shape[0]
    n_spans = len(outs) * n_slots
    heads = q_ref.shape[1] // HEAD
    rows = heads * SPAN
    wide = qs.shape[0]
    inv_root = 1.0 / math.sqrt(HEAD)
    scale2 = inv_root * math.log2(math.e)

    def span_at(entry):
        return pl.ds(pl.multiple_of(table_ref[entry] * SPAN, SPAN), SPAN)

    entry = 0
    for ref in blocks:
        for j in range(ref.shape[0]):
            for i in range(halves):
                kv_s[span_at(entry), :] = ref[j, i * SPAN : (i + 1) * SPAN]
                entry += 1

    def clear(p, carry):
        acc_s[pl.ds(pl.multiple_of(p * SPAN, SPAN), SPAN), :] = jnp.zeros(
            (SPAN, 2 * HEAD), jnp.float32
        )
        return carry

    lax.fori_loop(0, n_spans, clear, 0)
    qs[rows:, :] = jnp.zeros((wide - rows, HEAD), qs.dtype)
    gs[rows:, :] = jnp.zeros((wide - rows, HEAD), gs.dtype)

    for i in range(q_ref.shape[0] // SPAN):
        own = slice(i * SPAN, (i + 1) * SPAN)
        for h in range(heads):
            qs[h * SPAN : (h + 1) * SPAN, :] = q_ref[own, h * HEAD : (h + 1) * HEAD]
            gs[h * SPAN : (h + 1) * SPAN, :] = g_ref[own, h * HEAD : (h + 1) * HEAD]
        lo = table_ref[2 * n_spans + 2 * i]
        hi = table_ref[2 * n_spans + 2 * i + 1] + 1
        first = limit_ref[2 * i : 2 * i + 1, :]
        last = limit_ref[2 * i + 1 : 2 * i + 2, :]

        def block(b):
            return pl.ds(pl.multiple_of(b * BLOCK, BLOCK), BLOCK)

        def score(b, top):
            s = lax.dot_general(
                kv_s[block(b), :HEAD], qs[...], (((1,), (1,)), ((), ())),
                preferred_element_type=jnp.float32,
            ) * scale2
            pos = lax.broadcasted_iota(jnp.int32, s.shape, 0) + b * BLOCK
            s = jnp.where((pos >= first) & (pos <= last), s, MASKED)
            s_s[block(b), :] = s
            return jnp.maximum(top, jnp.max(s.reshape(BLOCK // 8, 8, wide), axis=0))

        top = lax.fori_loop(lo, hi, score, jnp.full((8, wide), MASKED, jnp.float32))
        top = jnp.max(top, axis=0, keepdims=True)

        def weigh(b, carry):
            total, summed = carry
            e = jnp.exp2(s_s[block(b), :] - top)
            s_s[block(b), :] = e
            total = total + jnp.sum(e.reshape(BLOCK // 8, 8, wide), axis=0)
            summed = summed + lax.dot_general(
                kv_s[block(b), HEAD:], e.astype(jnp.bfloat16), (((0,), (0,)), ((), ())),
                preferred_element_type=jnp.float32,
            )
            return total, summed

        total, summed = lax.fori_loop(
            lo, hi, weigh,
            (jnp.zeros((8, wide), jnp.float32), jnp.zeros((HEAD, wide), jnp.float32)),
        )
        share = 1.0 / jnp.sum(total, axis=0, keepdims=True)
        att = (summed * share).astype(jnp.bfloat16).astype(jnp.float32)
        delta = jnp.sum(att * gs[...].astype(jnp.float32).T, axis=0, keepdims=True)
        att = att.T.astype(jnp.bfloat16)

        def back(b, grad_q):
            k = kv_s[block(b), :HEAD]
            v = kv_s[block(b), HEAD:]
            p = s_s[block(b), :] * share
            grad_p = lax.dot_general(
                v, gs[...], (((1,), (1,)), ((), ())), preferred_element_type=jnp.float32
            )
            grad_s = (p * (grad_p - delta) * inv_root).astype(jnp.bfloat16)
            acc_s[block(b), HEAD:] += jnp.dot(
                p.astype(jnp.bfloat16), gs[...], preferred_element_type=jnp.float32
            )
            acc_s[block(b), :HEAD] += jnp.dot(
                grad_s, qs[...], preferred_element_type=jnp.float32
            )
            return grad_q + lax.dot_general(
                k, grad_s, (((0,), (0,)), ((), ())), preferred_element_type=jnp.float32
            )

        grad_q = lax.fori_loop(lo, hi, back, jnp.zeros((HEAD, wide), jnp.float32))
        grad_q = grad_q.T.astype(jnp.bfloat16)
        for h in range(heads):
            att_ref[own, h * HEAD : (h + 1) * HEAD] = att[h * SPAN : (h + 1) * SPAN]
            gq_ref[own, h * HEAD : (h + 1) * HEAD] = grad_q[h * SPAN : (h + 1) * SPAN]

    def send(j, carry):
        for k, out in enumerate(outs):
            out[j] = acc_s[span_at(n_spans + k * n_slots + j), :].astype(jnp.bfloat16)
        return carry

    lax.fori_loop(0, n_slots, send, 0)


def attend(table, limit, queries, grads, near, far):
    smem = pl.BlockSpec(memory_space=pltpu.SMEM)
    vmem = pl.BlockSpec(memory_space=pltpu.VMEM)
    shard = queries.shape[0]
    n_slots = sum(x.shape[0] for x in near) // 2
    tokens = 4 * n_slots * shard
    wide = limit.shape[1]
    part = jax.ShapeDtypeStruct((n_slots, SPAN, 2 * HEAD), jnp.bfloat16)
    rows_like = jax.ShapeDtypeStruct(queries.shape, jnp.bfloat16)
    return pl.pallas_call(
        functools.partial(attention_kernel, len(near)),
        name="attention",
        out_shape=(rows_like, rows_like) + (part,) * 8,
        in_specs=[smem] + [vmem] * (3 + len(near) + len(far)),
        out_specs=[vmem] * 10,
        scratch_shapes=[
            pltpu.VMEM((tokens, 2 * HEAD), jnp.bfloat16),
            pltpu.VMEM((tokens, 2 * HEAD), jnp.float32),
            pltpu.VMEM((tokens, wide), jnp.float32),
            pltpu.VMEM((wide, HEAD), jnp.bfloat16),
            pltpu.VMEM((wide, HEAD), jnp.bfloat16),
        ],
    )(table, limit, queries, grads, *near, *far)


def strips_kernel(at_ref, rows_ref, keep_ref, give_c_ref, give_x_ref, turned):
    n_z, part, _ = keep_ref.shape
    for i in range(n_z):
        turned[...] = rows_ref[:, i * 4 * part : (i + 1) * 4 * part].astype(jnp.float32).T
        for ref, slot, k in (
            (keep_ref, i, 0),
            (give_c_ref, i, 1),
            (give_x_ref, i, 2),
            (give_c_ref, n_z + i, 3),
        ):
            start = pl.multiple_of(at_ref[k] * part, 16)
            ref[slot] = turned[pl.ds(start, part), :].astype(jnp.bfloat16)


def strips_of(at, rows, n_z):
    shard, width = rows.shape
    part = width // (4 * n_z)
    vmem = pl.BlockSpec(memory_space=pltpu.VMEM)

    def like(n):
        return jax.ShapeDtypeStruct((n, part, shard), jnp.bfloat16)

    return pl.pallas_call(
        strips_kernel,
        name="strips",
        out_shape=(like(n_z), like(2 * n_z), like(n_z)),
        in_specs=[pl.BlockSpec(memory_space=pltpu.SMEM), vmem],
        out_specs=[vmem] * 3,
        scratch_shapes=[pltpu.VMEM((4 * part, shard), jnp.float32)],
    )(at, rows)


def grad_w_kernel(z_ref, a_ref, b_ref, c_ref, d_ref, own_ref, far_ref, side_ref, own_out, *outs):
    n_z = a_ref.shape[0]
    for k, out in enumerate((own_out, *outs)):
        i = lax.rem(z_ref[0] + k, n_z)
        total = jnp.dot(a_ref[i], own_ref[...], preferred_element_type=jnp.float32)
        total += jnp.dot(b_ref[i], far_ref[0], preferred_element_type=jnp.float32)
        total += jnp.dot(c_ref[i], side_ref[...], preferred_element_type=jnp.float32)
        total += jnp.dot(d_ref[i], far_ref[1], preferred_element_type=jnp.float32)
        out[...] = total.astype(out.dtype)


def grad_w_parts(z, strips, own, far, side):
    n_z, part, _ = strips[0].shape
    vmem = pl.BlockSpec(memory_space=pltpu.VMEM)
    shape = (part, own.shape[1])
    return pl.pallas_call(
        grad_w_kernel,
        name="grad_w",
        out_shape=(jax.ShapeDtypeStruct(shape, jnp.float32),)
        + (jax.ShapeDtypeStruct(shape, jnp.bfloat16),) * (n_z - 1),
        in_specs=[pl.BlockSpec(memory_space=pltpu.SMEM)] + [vmem] * 7,
        out_specs=[vmem] * n_z,
    )(z, *strips, own, far, side)


def on_device(
    n_z, activations, queries, key_weight, value_weight, output_gradient, span_order, doc_ids
):
    n_ten = 8
    own_rows, width = activations.shape
    shard = own_rows * n_ten
    spans = span_order.shape[0]
    per_shard = shard // SPAN
    heads = queries.shape[1] // HEAD
    z, xl, c = (lax.axis_index(a) for a in CTX)
    swap = [(0, 1), (1, 0)]
    up = [(i, (i + 1) % n_z) for i in range(n_z)]
    down = [(i, (i - 1) % n_z) for i in range(n_z)]

    dz = jnp.array([d for d, _ in brought(n_z)], jnp.int32)
    side = jnp.array([x for _, x in brought(n_z)], jnp.int32)
    halves = jnp.arange(per_shard, dtype=jnp.int32)
    in_near = (((z - dz) % n_z) * 4 + (xl ^ side) * 2)[:, None] * per_shard + halves[None, :]
    out_z = jnp.arange(n_z, dtype=jnp.int32)
    out_side = xl ^ jnp.arange(2, dtype=jnp.int32)
    out_near = (out_z[None, None, :] * 4 + out_side[None, :, None] * 2) * per_shard
    out_near = out_near + halves[:, None, None]
    spans_of = jnp.concatenate(
        [
            (in_near + c * per_shard).reshape(-1),
            (in_near + (1 - c) * per_shard).reshape(-1),
            (out_near + c * per_shard).reshape(-1),
            (out_near + (1 - c) * per_shard).reshape(-1),
        ]
    )
    ids = jnp.arange(spans, dtype=jnp.int32)
    places = jnp.sum(jnp.where(spans_of[:, None] == ids[None, :], span_order[None, :], 0), axis=1)
    first_row = (z * 4 + xl * 2 + c) * shard
    my_order = lax.dynamic_slice_in_dim(span_order, first_row // SPAN, per_shard)
    my_doc = lax.dynamic_slice_in_dim(doc_ids, first_row, shard)
    my_first = jnp.sum((doc_ids[None, :] < my_doc[:, None]).astype(jnp.int32), axis=1)
    my_first = my_first.reshape(per_shard, SPAN)
    my_pos = my_order[:, None] * SPAN + jnp.arange(SPAN, dtype=jnp.int32)[None, :]
    bound = jnp.stack([jnp.min(my_first, axis=1) // BLOCK, my_pos[:, -1] // BLOCK], axis=1)
    table = jnp.concatenate([places, bound.reshape(-1)])
    wide = -(-heads * SPAN // 128) * 128
    pad = wide - heads * SPAN
    limit = jnp.stack(
        [
            jnp.pad(jnp.tile(my_first, (1, heads)), ((0, 0), (0, pad)), constant_values=1),
            jnp.pad(jnp.tile(my_pos, (1, heads)), ((0, 0), (0, pad))),
        ],
        axis=1,
    ).reshape(2 * per_shard, wide)

    def low(x):
        return x.astype(jnp.bfloat16)

    def add(x, y):
        return low(x.astype(jnp.float32) + y.astype(jnp.float32))

    rows = lax.all_to_all(
        jnp.broadcast_to(activations[None], (n_ten, own_rows, width)), TEN, 0, 0
    ).reshape(shard, width)
    rows, table, limit = lax.optimization_barrier((rows, table, limit))
    kv = jnp.concatenate(
        [
            low(jnp.dot(rows, w, preferred_element_type=jnp.float32))
            for w in (key_weight, value_weight)
        ],
        axis=1,
    )
    pair = jnp.stack([kv, lax.ppermute(kv, "xl", swap)])
    pair, rows = lax.optimization_barrier((pair, rows))
    near = [pair]
    a = b = pair
    for _ in range(1, n_z // 2):
        a = lax.ppermute(a, "z", up)
        b = lax.ppermute(b, "z", down)
        near += [a, b]
    near.append(lax.ppermute(a[:1], "z", up))
    near.append(lax.ppermute(b[1:], "z", down))
    far = [lax.ppermute(x, "c", swap) for x in near]

    around = jnp.stack([xl * 2 + c, xl * 2 + 1 - c, (1 - xl) * 2 + c, (1 - xl) * 2 + 1 - c])
    keep, give_c, give_x = strips_of(around, rows, n_z)
    got_c = lax.ppermute(give_c, "c", swap)
    got_x = lax.ppermute(give_x, "xl", swap)
    got_cx = lax.ppermute(got_c[n_z:], "xl", swap)
    strips = (keep, got_c[:n_z], got_x, got_cx)

    attended, grad_queries, *parts = attend(
        table, limit, queries, output_gradient, near, far
    )

    own = []
    for i in range(per_shard):
        near_0, near_1 = parts[2 * i : 2 * i + 2]
        far_0, far_1 = parts[2 * per_shard + 2 * i : 2 * per_shard + 2 * i + 2]
        far_1 = lax.ppermute(far_1, "c", swap)
        far_0 = lax.ppermute(far_0, "c", swap)
        part = lax.ppermute(add(near_1, far_1), "xl", swap)
        part = low(near_0.astype(jnp.float32) + far_0.astype(jnp.float32) + part.astype(jnp.float32))
        part = lax.all_to_all(part, "z", 0, 0)
        own.append(low(jnp.sum(part.astype(jnp.float32), axis=0)))
    grad_kv = jnp.concatenate(own, axis=0)

    beside = lax.ppermute(grad_kv, "xl", swap)
    grad_rows = lax.dot_general(
        grad_kv[:, :HEAD], key_weight, (((1,), (1,)), ((), ())), preferred_element_type=jnp.float32
    ) + lax.dot_general(
        grad_kv[:, HEAD:], value_weight, (((1,), (1,)), ((), ())),
        preferred_element_type=jnp.float32,
    )
    grad_rows, beside = lax.optimization_barrier((low(grad_rows), beside))
    terms = lax.all_to_all(grad_rows.reshape(n_ten, own_rows, width), TEN, 0, 0)

    both = jnp.stack([grad_kv, beside])
    across = lax.ppermute(both, "c", swap)
    grad_w, *sent = grad_w_parts(z[None], strips, grad_kv, across, beside)
    for k, x in enumerate(sent, 1):
        shift = [(i, (i + k) % n_z) for i in range(n_z)]
        grad_w = grad_w + lax.ppermute(x, "z", shift).astype(jnp.float32)
    grad_inputs = low(jnp.sum(terms.astype(jnp.float32), axis=0))
    return attended, grad_queries, grad_inputs, grad_w[:, :HEAD], grad_w[:, HEAD:]


def solution(mesh):
    n_z = mesh.shape["context"] // 4
    fine = Mesh(mesh.devices.reshape(n_z, 2, 2, 2, 4), CTX + TEN)

    def body(*args):
        return on_device(n_z, *args)

    return jax.shard_map(
        body,
        mesh=fine,
        in_specs=(
            P(CTX + TEN, None),
            P(CTX, TEN),
            P(None, TEN),
            P(None, TEN),
            P(CTX, TEN),
            P(),
            P(),
        ),
        out_specs=(
            P(CTX, TEN),
            P(CTX, TEN),
            P(CTX + TEN, None),
            P(CTX, TEN),
            P(CTX, TEN),
        ),
        check_vma=False,
    )
```

time: 702 us -> 241 us (0.34)
  waiting for transfers between devices: 573 us -> 123 us
  matrix products: 83.9 us -> 6.03 us
  starting transfers between devices: 0.28 us -> 69.2 us
  Pallas kernels: 0 us -> 20.4 us
  between operations: 14.3 us -> 1.06 us
    reduce_scatter x3 -> x0, waiting for transfers between devices: 309 us -> none  [the longest x1 120 us: on_device(): lax.psum_scatter(grad_v_buf.astype(jnp.bfloat16), 'context', scatter_dime...]
    all_gather x3 -> x0, waiting for transfers between devices: 155 us -> none  [the longest x1 62.8 us: on_device(): local_rows = lax.all_gather(activations, 'tensor', axis=0, tiled=True)]
    unnamed x8 -> x0, waiting for transfers between devices: 109 us -> none
    ppermute x0 -> x36, waiting for transfers between devices: none -> 92.8 us  [the longest x1 33.6 us: on_device(): got_x = lax.ppermute(give_x, 'xl', swap)]
    dot_general x11 -> x4, matrix products: 83.9 us -> 6.03 us  [the longest x2 3.35 us: on_device(): jnp.dot(rows, w, preferred_element_type=jnp.float32)]
    ppermute x0 -> x36, starting transfers between devices: none -> 39.7 us  [the longest x7 13.3 us: on_device(): grad_w = grad_w + lax.ppermute(x, 'z', shift).astype(jnp.float32)]
    all_to_all x0 -> x4, waiting for transfers between devices: none -> 30.2 us  [the longest x1 21.6 us: on_device(): lax.all_to_all(jnp.broadcast_to(activations[None], (n_ten, own_rows, widt...]
    all_to_all x0 -> x4, starting transfers between devices: none -> 29.5 us  [the longest x2 17.4 us: on_device(): part = lax.all_to_all(part, 'z', 0, 0)]
  transfers between devices with their start and end apart: 7 -> 40, of which waited for: 7 -> 21; matrix products, arithmetic and copies ran while one was open for 9% -> 6% of each run, Pallas kernels for 0% -> 3%
where the time goes in v1:
time: 241 us; the launch traced here: 239 us
  waiting for transfers between devices  123 us (51%)
  starting transfers between devices  69.2 us (29%)
  Pallas kernels  20.4 us (8%)
  local copies, waits for them, and re-layouts  9.92 us (4%)
  other arithmetic  9.28 us (4%)
  matrix products  6.03 us (3%)
    ppermute x1, waiting for transfers between devices, on_device(): got_x = lax.ppermute(give_x, 'xl', swap)  33.6 us
    all_to_all x1, waiting for transfers between devices, on_device(): lax.all_to_all(jnp.broadcast_to(activations[None], (n_ten, own_rows, widt...  21.6 us
    ppermute x2, waiting for transfers between devices, on_device(): part = lax.ppermute(add(near_1, far_1), 'xl', swap)  18.6 us
    all_to_all x2, starting transfers between devices, on_device(): part = lax.all_to_all(part, 'z', 0, 0)  17.4 us
    ppermute x7, starting transfers between devices, on_device(): grad_w = grad_w + lax.ppermute(x, 'z', shift).astype(jnp.float32)  13.3 us
    pallas_call x1, Pallas kernels, attend(): pl.pallas_call(functools.partial(attention_kernel, len(near)), name='atte...  13.1 us
    ppermute x3, waiting for transfers between devices, on_device(): a = lax.ppermute(a, 'z', up)  10.2 us
    all_to_all x2, waiting for transfers between devices, on_device(): part = lax.all_to_all(part, 'z', 0, 0)  8.58 us
  transfers between devices with their start and end apart: 40, of which 21 were waited for; matrix products, arithmetic and copies ran while one was open for 6% of the time, Pallas kernels for 3%

profile of v1, /device:TPU:32, one launch (start us, length us, event | category | flops | bytes accessed | tf_op | source)
XLA Modules:
  0.0 238.8 jit_solution(9526638327322072270)
XLA Ops:
  0.6 2.6 %broadcast_in_dim.16 = bf16[8,24,5120]{2,1,0:T(8,128)(2,1)} broadcast(bf16[24,5120]{1,0:T(8,128)(2,1)} %param.9), dimensions={1,2} | broadcast | bytes 2211840 | tf_op jit(solution)/shard_map/broadcast_in_dim | solution.py:277
  3.2 7.1 %all-to-all-start = ((bf16[8,24,5120]{2,1,0:T(8,128)(2,1)}), bf16[8,24,5120]{2,1,0:T(8,128)(2,1)S(1)}, u32[]{:S(2)}, u32[]{:S(2)}) async-start(bf16[8,24,5120]{2,1,0:T(8,128)(2,1)} %broadcast_in_dim.16), calls=%async_computation | async-start | bytes 3932160 | tf_op jit(solution)/shard_map/all_to_all | solution.py:276
  10.7 0.6 convert_reduce_fusion
  11.5 0.6 reshape.165.limit_ref
  13.7 21.6 %all-to-all-done = bf16[8,24,5120]{2,1,0:T(8,128)(2,1)S(1)} async-done(((bf16[8,24,5120]{2,1,0:T(8,128)(2,1)}), bf16[8,24,5120]{2,1,0:T(8,128)(2,1)S(1)}, u32[]{:S(2)}, u32[]{:S(2)}) %all-to-all-start) | async-done | bytes 1966112 | tf_op jit(solution)/shard_map/all_to_all | solution.py:276
  35.3 2.7 %convolution_convert_fusion = bf16[192,128]{1,0:T(8,128)(2,1)S(1)} fusion(bf16[192,5120]{1,0:T(8,128)(2,1)S(1)} %bitcast.27, bf16[5120,128]{1,0:T(8,128)(2,1)} %param.12), kind=kOutput, calls=%fused_computation.3 | convolution fusion | flops 251682816 | bytes 3325952 | tf_op jit(solution)/shard_map/dot_general | solution.py:282
  38.0 0.7 convolution_convert_fusion.1
  38.7 0.7 collective-permute-start
  39.4 4.0 %collective-permute-done = bf16[192,256]{1,0:T(8,128)(2,1)S(1)} collective-permute-done((bf16[192,256]{1,0:T(8,128)(2,1)S(1)}, bf16[192,256]{1,0:T(8,128)(2,1)S(1)}, u32[]{:S(2)}, u32[]{:S(2)}) %collective-permute-start) | collective-permute-done | bytes 98336 | tf_op jit(solution)/shard_map/ppermute | solution.py:287
  43.5 2.0 collective-permute-start.1
  45.6 3.6 %collective-permute-done.1.refs_1_ = bf16[2,192,256]{2,1,0:T(8,128)(2,1)S(1)} collective-permute-done((bf16[2,192,256]{2,1,0:T(8,128)(2,1)S(1)}, bf16[2,192,256]{2,1,0:T(8,128)(2,1)S(1)}, u32[]{:S(2)}, u32[]{:S(2)}) %collective-permute-start.1) | collective-permute-done | bytes 196640 | tf_op jit(solution)/shard_map/ppermute | solution.py:292
  49.2 2.3 collective-permute-start.3
  51.5 1.8 collective-permute-start.4
  53.3 3.5 %collective-permute-done.3.refs_3_ = bf16[2,192,256]{2,1,0:T(8,128)(2,1)S(1)} collective-permute-done((bf16[2,192,256]{2,1,0:T(8,128)(2,1)S(1)}, bf16[2,192,256]{2,1,0:T(8,128)(2,1)S(1)}, u32[]{:S(2)}, u32[]{:S(2)}) %collective-permute-start.3) | collective-permute-done | bytes 196640 | tf_op jit(solution)/shard_map/ppermute | solution.py:292
  56.8 1.4 collective-permute-start.5
  58.2 2.0 collective-permute-start.6
  60.7 3.0 %collective-permute-done.5.refs_5_ = bf16[2,192,256]{2,1,0:T(8,128)(2,1)S(1)} collective-permute-done((bf16[2,192,256]{2,1,0:T(8,128)(2,1)S(1)}, bf16[2,192,256]{2,1,0:T(8,128)(2,1)S(1)}, u32[]{:S(2)}, u32[]{:S(2)}) %collective-permute-start.5) | collective-permute-done | bytes 196640 | tf_op jit(solution)/shard_map/ppermute | solution.py:292
  63.7 1.3 collective-permute-done.6.refs_6_
  65.0 3.6 %collective-permute-start.7 = (bf16[1,192,256]{2,1,0:T(8,128)(2,1)S(1)}, bf16[1,192,256]{2,1,0:T(8,128)(2,1)S(1)}, u32[]{:S(2)}, u32[]{:S(2)}) collective-permute-start(bf16[1,192,256]{2,1,0:T(8,128)(2,1)S(1)} %slice.37), channel_id=1, source_target_pairs={{0,32},{32,64},{64,96},{96,128},{128,160},{160,192},{192,224},{224... | collective-permute-start | bytes 294920 | tf_op jit(solution)/shard_map/ppermute | solution.py:295
  69.3 2.1 collective-permute-done.7.refs_7_
  71.4 3.7 %collective-permute-done.8.refs_8_ = bf16[1,192,256]{2,1,0:T(8,128)(2,1)S(1)} collective-permute-done((bf16[1,192,256]{2,1,0:T(8,128)(2,1)S(1)}, bf16[1,192,256]{2,1,0:T(8,128)(2,1)S(1)}, u32[]{:S(2)}, u32[]{:S(2)}) %collective-permute-start.8) | collective-permute-done | bytes 98336 | tf_op jit(solution)/shard_map/ppermute | solution.py:296
  75.1 1.3 collective-permute-done.17.refs_17_
  77.0 0.7 copy-done.23
  77.8 13.1 %attention.1 = (bf16[192,640]{1,0:T(8,128)(2,1)}, bf16[192,640]{1,0:T(8,128)(2,1)}, bf16[8,96,256]{2,1,0:T(8,128)(2,1)}, bf16[8,96,256]{2,1,0:T(8,128)(2,1)}, bf...) custom-call(s32[132]{0:T(256)} %pad_add_fusion.2.table_ref, ...), custom_call_target="tpu_custom_call" | custom-call | tf_op jit(solution)/shard_map/attention/pallas_call | solution.py:147
  90.9 3.8 %collective-permute-start.22 = (bf16[8,96,256]{2,1,0:T(8,128)(2,1)}, bf16[8,96,256]{2,1,0:T(8,128)(2,1)S(1)}, u32[]{:S(2)}, u32[]{:S(2)}) collective-permute-start(bf16[8,96,256]{2,1,0:T(8,128)(2,1)} %get-tuple-element.46), channel_id=1, source_target_pairs={{0,8},{8,0},{1,9},{9,1},{2,10},{10,2},{3,11},{11,3},{4,12},{12,4},... | collective-permute-start | bytes 1179656 | tf_op jit(solution)/shard_map/ppermute | solution.py:314
  94.8 1.5 collective-permute-done.22
  96.3 1.1 add_convert_fusion.1
  97.4 3.3 %collective-permute-start.23 = (bf16[8,96,256]{2,1,0:T(8,128)(2,1)S(1)}, bf16[8,96,256]{2,1,0:T(8,128)(2,1)S(1)}, u32[]{:S(2)}, u32[]{:S(2)}) collective-permute-start(bf16[8,96,256]{2,1,0:T(8,128)(2,1)S(1)} %add_convert_fusion.1), channel_id=1, source_target_pairs={{0,16},{16,0},{1,17},{17,1},{2,18},{18,2},{3,19},{19,3},{4,20},{20... | collective-permute-start | bytes 1179656 | tf_op jit(solution)/shard_map/ppermute | solution.py:316
  101.2 8.9 %collective-permute-done.23 = bf16[8,96,256]{2,1,0:T(8,128)(2,1)S(1)} collective-permute-done((bf16[8,96,256]{2,1,0:T(8,128)(2,1)S(1)}, bf16[8,96,256]{2,1,0:T(8,128)(2,1)S(1)}, u32[]{:S(2)}, u32[]{:S(2)}) %collective-permute-start.23) | collective-permute-done | bytes 393248 | tf_op jit(solution)/shard_map/ppermute | solution.py:316
  110.1 1.9 add_convert_fusion
  112.0 12.0 %all-to-all-start.2 = ((bf16[8,96,256]{2,1,0:T(8,128)(2,1)}), bf16[8,96,256]{2,1,0:T(8,128)(2,1)S(1)}, u32[]{:S(2)}, u32[]{:S(2)}) async-start(bf16[8,96,256]{2,1,0:T(8,128)(2,1)} %add_convert_fusion), calls=%async_computation.2 | async-start | bytes 786432 | tf_op jit(solution)/shard_map/all_to_all | solution.py:318
  124.4 9.7 %collective-permute-done.20 = bf16[8,96,256]{2,1,0:T(8,128)(2,1)S(1)} collective-permute-done((bf16[8,96,256]{2,1,0:T(8,128)(2,1)S(1)}, bf16[8,96,256]{2,1,0:T(8,128)(2,1)S(1)}, u32[]{:S(2)}, u32[]{:S(2)}) %collective-permute-start.20) | collective-permute-done | bytes 393248 | tf_op jit(solution)/shard_map/ppermute | solution.py:316
  134.1 0.9 add_convert_fusion.2
  135.0 1.8 all-to-all-done.2
  136.9 5.4 %all-to-all-start.1 = ((bf16[8,96,256]{2,1,0:T(8,128)(2,1)}), bf16[8,96,256]{2,1,0:T(8,128)(2,1)S(1)}, u32[]{:S(2)}, u32[]{:S(2)}) async-start(bf16[8,96,256]{2,1,0:T(8,128)(2,1)} %add_convert_fusion.2), calls=%async_computation.1 | async-start | bytes 786432 | tf_op jit(solution)/shard_map/all_to_all | solution.py:318
  142.2 0.7 pad_add_fusion.4.at_ref
  142.9 4.0 %strips.1 = (bf16[8,160,192]{2,1,0:T(8,128)(2,1)}, bf16[16,160,192]{2,1,0:T(8,128)(2,1)}, bf16[8,160,192]{2,1,0:T(8,128)(2,1)}) custom-call(s32[4]{0:T(128)} %pad_add_fusion.4.at_ref, bf16[192,5120]{1,0:T(8,128)(2,1)} %bitcast.29), custom_call_target="tpu_custom_call" | custom-call | tf_op jit(solution)/shard_map/strips/pallas_call | solution.py:185
  147.0 6.8 %all-to-all-done.1 = bf16[8,96,256]{2,1,0:T(8,128)(2,1)S(1)} async-done(((bf16[8,96,256]{2,1,0:T(8,128)(2,1)}), bf16[8,96,256]{2,1,0:T(8,128)(2,1)S(1)}, u32[]{:S(2)}, u32[]{:S(2)}) %all-to-all-start.1) | async-done | bytes 393248 | tf_op jit(solution)/shard_map/all_to_all | solution.py:318
  153.8 0.7 fusion.17
  154.5 1.3 collective-permute-start.24
  155.7 0.7 fusion.2
  156.4 2.0 fusion
  158.4 0.7 collective-permute-done.24.side_ref
  159.1 5.0 %all-to-all-start.3 = ((bf16[8,24,5120]{2,1,0:T(8,128)(2,1)}), bf16[8,24,5120]{2,1,0:T(8,128)(2,1)S(1)}, u32[]{:S(2)}, u32[]{:S(2)}) async-start(bf16[8,24,5120]{2,1,0:T(8,128)(2,1)} %bitcast.7), calls=%async_computation.3 | async-start | bytes 3932160 | tf_op jit(solution)/shard_map/all_to_all | solution.py:330
  164.1 1.3 collective-permute-start.26
  165.4 2.2 fusion.18
  167.6 0.9 collective-permute-start.27
  168.6 33.6 %collective-permute-done.26.c_ref = bf16[8,160,192]{2,1,0:T(8,128)(2,1)S(1)} collective-permute-done((bf16[8,160,192]{2,1,0:T(8,128)(2,1)}, bf16[8,160,192]{2,1,0:T(8,128)(2,1)S(1)}, u32[]{:S(2)}, u32[]{:S(2)}) %collective-permute-start.26) | collective-permute-done | bytes 491552 | tf_op jit(solution)/shard_map/ppermute | solution.py:302
  202.1 8.3 %collective-permute-done.27.d_ref = bf16[8,160,192]{2,1,0:T(8,128)(2,1)S(1)} collective-permute-done((bf16[8,160,192]{2,1,0:T(8,128)(2,1)S(1)}, bf16[8,160,192]{2,1,0:T(8,128)(2,1)S(1)}, u32[]{:S(2)}, u32[]{:S(2)}) %collective-permute-start.27) | collective-permute-done | bytes 491552 | tf_op jit(solution)/shard_map/ppermute | solution.py:303
  210.5 0.8 copy-done.5
  211.3 0.7 copy-done.13
  212.0 3.3 %grad_w.1 = (f32[160,256]{1,0:T(8,128)}, bf16[160,256]{1,0:T(8,128)(2,1)}, bf16[160,256]{1,0:T(8,128)(2,1)}, bf16[160,256]{1,0:T(8,128)(2,1)}, bf16[160,256]{1,0...) custom-call(s32[1]{0:T(128)} %bitcast.8.z_ref, ...), custom_call_target="tpu_custom_call" | custom-call | tf_op jit(solution)/shard_map/grad_w/pallas_call | solution.py:210
  215.3 1.7 collective-permute-start.29
  217.0 1.4 collective-permute-start.30
  218.4 2.3 collective-permute-start.31
  220.7 3.2 %collective-permute-start.32 = (bf16[160,256]{1,0:T(8,128)(2,1)}, bf16[160,256]{1,0:T(8,128)(2,1)S(1)}, u32[]{:S(2)}, u32[]{:S(2)}) collective-permute-start(bf16[160,256]{1,0:T(8,128)(2,1)} %get-tuple-element.57), channel_id=1, source_target_pairs={{0,128},{32,160},{64,192},{96,224},{128,0},{160,32},{192,64},{224,... | collective-permute-start | bytes 245768 | tf_op jit(solution)/shard_map/ppermute | solution.py:337
  223.9 3.7 %collective-permute-start.33 = (bf16[160,256]{1,0:T(8,128)(2,1)}, bf16[160,256]{1,0:T(8,128)(2,1)S(1)}, u32[]{:S(2)}, u32[]{:S(2)}) collective-permute-start(bf16[160,256]{1,0:T(8,128)(2,1)} %get-tuple-element.58), channel_id=1, source_target_pairs={{0,160},{32,192},{64,224},{96,0},{128,32},{160,64},{192,96},{224,1... | collective-permute-start | bytes 245768 | tf_op jit(solution)/shard_map/ppermute | solution.py:337
  227.6 1.0 collective-permute-start.34
  228.6 2.1 collective-permute-done.31
  230.7 0.8 collective-permute-done.32
  231.6 4.2 %collective-permute-done.33 = bf16[160,256]{1,0:T(8,128)(2,1)S(1)} collective-permute-done((bf16[160,256]{1,0:T(8,128)(2,1)}, bf16[160,256]{1,0:T(8,128)(2,1)S(1)}, u32[]{:S(2)}, u32[]{:S(2)}) %collective-permute-start.33) | collective-permute-done | bytes 81952 | tf_op jit(solution)/shard_map/ppermute | solution.py:337
  236.2 1.0 convert_add_fusion
  237.2 0.7 fusion.19
  237.8 1.0 reduce_sum.58
  (137 shorter events, 5.9 us)
Async XLA Ops:
  0.6 37.4 %copy-start = (bf16[5120,128]{1,0:T(8,128)(2,1)S(1)}, bf16[5120,128]{1,0:T(8,128)(2,1)}, u32[]{:S(2)}) copy-start(bf16[5120,128]{1,0:T(8,128)(2,1)} %param.11) | copy-start | bytes 3932164
  3.2 7.1 %copy-start.31 = (s32[64]{0:T(128)S(1)}, s32[64]{0:T(128)}, u32[]{:S(2)}) copy-start(s32[64]{0:T(128)} %param.14) | copy-start | bytes 772
  3.2 7.3 %copy-start.28 = (s32[6144]{0:T(1024)S(1)}, s32[6144]{0:T(1024)}, u32[]{:S(2)}) copy-start(s32[6144]{0:T(1024)} %param.15) | copy-start | bytes 73732
  3.2 9.2 %copy-start.29 = (s32[16]{0:T(128)S(1)}, s32[16]{0:T(128)}, u32[]{:S(2)}) copy-start(s32[16]{0:T(128)} %constant.82.clone) | copy-start | bytes 196
  3.2 9.2 %copy-start.30 = (s32[16]{0:T(128)S(1)}, s32[16]{0:T(128)}, u32[]{:S(2)}) copy-start(s32[16]{0:T(128)} %constant.88) | copy-start | bytes 196
  3.2 32.1 %all-to-all-start = ((bf16[8,24,5120]{2,1,0:T(8,128)(2,1)}), bf16[8,24,5120]{2,1,0:T(8,128)(2,1)S(1)}, u32[]{:S(2)}, u32[]{:S(2)}) async-start(bf16[8,24,5120]{2,1,0:T(8,128)(2,1)} %broadcast_in_dim.16), calls=%async_computation | async-start | bytes 3932160 | tf_op jit(solution)/shard_map/all_to_all | solution.py:276
  35.3 3.4 %copy-start.1 = (bf16[8,24,5120]{2,1,0:T(8,128)(2,1)}, bf16[8,24,5120]{2,1,0:T(8,128)(2,1)S(1)}, u32[]{:S(2)}) copy-start(bf16[8,24,5120]{2,1,0:T(8,128)(2,1)S(1)} %all-to-all-done) | copy-start | bytes 5898244
  38.7 4.7 %collective-permute-start = (bf16[192,256]{1,0:T(8,128)(2,1)S(1)}, bf16[192,256]{1,0:T(8,128)(2,1)S(1)}, u32[]{:S(2)}, u32[]{:S(2)}) collective-permute-start(bf16[192,256]{1,0:T(8,128)(2,1)S(1)} %get-tuple-element.68), channel_id=1, source_target_pairs={{0,16},{16,0},{1,17},{17,1},{2,18},{18,2},{3,19},{19,3},{4,20},{20... | collective-permute-start | bytes 294920 | tf_op jit(solution)/shard_map/ppermute | solution.py:287
  43.5 34.2 %copy-start.3 = (bf16[2,192,256]{2,1,0:T(8,128)(2,1)}, bf16[2,192,256]{2,1,0:T(8,128)(2,1)S(1)}, u32[]{:S(2)}) copy-start(bf16[2,192,256]{2,1,0:T(8,128)(2,1)S(1)} %pad_maximum_fusion.refs_0_) | copy-start | bytes 589828
  43.5 5.7 %collective-permute-start.1 = (bf16[2,192,256]{2,1,0:T(8,128)(2,1)S(1)}, bf16[2,192,256]{2,1,0:T(8,128)(2,1)S(1)}, u32[]{:S(2)}, u32[]{:S(2)}) collective-permute-start(bf16[2,192,256]{2,1,0:T(8,128)(2,1)S(1)} %pad_maximum_fusion.refs_0_), channel_id=1, source_target_pairs={{0,32},{32,64},{64,96},{96,128},{128,160},{160,192},{192,224},{224... | collective-permute-start | bytes 589832 | tf_op jit(solution)/shard_map/ppermute | solution.py:292
  45.5 6.0 %collective-permute-start.2 = (bf16[2,192,256]{2,1,0:T(8,128)(2,1)S(1)}, bf16[2,192,256]{2,1,0:T(8,128)(2,1)S(1)}, u32[]{:S(2)}, u32[]{:S(2)}) collective-permute-start(bf16[2,192,256]{2,1,0:T(8,128)(2,1)S(1)} %pad_maximum_fusion.refs_0_), channel_id=1, source_target_pairs={{0,224},{32,0},{64,32},{96,64},{128,96},{160,128},{192,160},{224,1... | collective-permute-start | bytes 589832 | tf_op jit(solution)/shard_map/ppermute | solution.py:293
  49.2 28.4 %copy-start.14 = (bf16[2,192,256]{2,1,0:T(8,128)(2,1)}, bf16[2,192,256]{2,1,0:T(8,128)(2,1)S(1)}, u32[]{:S(2)}) copy-start(bf16[2,192,256]{2,1,0:T(8,128)(2,1)S(1)} %collective-permute-done.1.refs_1_) | copy-start | bytes 589828
  49.2 7.6 %collective-permute-start.3 = (bf16[2,192,256]{2,1,0:T(8,128)(2,1)S(1)}, bf16[2,192,256]{2,1,0:T(8,128)(2,1)S(1)}, u32[]{:S(2)}, u32[]{:S(2)}) collective-permute-start(bf16[2,192,256]{2,1,0:T(8,128)(2,1)S(1)} %collective-permute-done.1.refs_1_), channel_id=1, source_target_pairs={{0,32},{32,64},{64,96},{96,128},{128,160},{160,192},{192,224},{224... | collective-permute-start | bytes 589832 | tf_op jit(solution)/shard_map/ppermute | solution.py:292
  51.5 26.2 %copy-start.15 = (bf16[2,192,256]{2,1,0:T(8,128)(2,1)}, bf16[2,192,256]{2,1,0:T(8,128)(2,1)S(1)}, u32[]{:S(2)}) copy-start(bf16[2,192,256]{2,1,0:T(8,128)(2,1)S(1)} %collective-permute-done.2.refs_2_) | copy-start | bytes 589828
  51.5 6.7 %collective-permute-start.4 = (bf16[2,192,256]{2,1,0:T(8,128)(2,1)S(1)}, bf16[2,192,256]{2,1,0:T(8,128)(2,1)S(1)}, u32[]{:S(2)}, u32[]{:S(2)}) collective-permute-start(bf16[2,192,256]{2,1,0:T(8,128)(2,1)S(1)} %collective-permute-done.2.refs_2_), channel_id=1, source_target_pairs={{0,224},{32,0},{64,32},{96,64},{128,96},{160,128},{192,160},{224,1... | collective-permute-start | bytes 589832 | tf_op jit(solution)/shard_map/ppermute | solution.py:293
  56.8 20.9 %copy-start.16 = (bf16[2,192,256]{2,1,0:T(8,128)(2,1)}, bf16[2,192,256]{2,1,0:T(8,128)(2,1)S(1)}, u32[]{:S(2)}) copy-start(bf16[2,192,256]{2,1,0:T(8,128)(2,1)S(1)} %collective-permute-done.3.refs_3_) | copy-start | bytes 589828
  56.8 6.9 %collective-permute-start.5 = (bf16[2,192,256]{2,1,0:T(8,128)(2,1)S(1)}, bf16[2,192,256]{2,1,0:T(8,128)(2,1)S(1)}, u32[]{:S(2)}, u32[]{:S(2)}) collective-permute-start(bf16[2,192,256]{2,1,0:T(8,128)(2,1)S(1)} %collective-permute-done.3.refs_3_), channel_id=1, source_target_pairs={{0,32},{32,64},{64,96},{96,128},{128,160},{160,192},{192,224},{224... | collective-permute-start | bytes 589832 | tf_op jit(solution)/shard_map/ppermute | solution.py:292
  58.2 19.5 %copy-start.17 = (bf16[2,192,256]{2,1,0:T(8,128)(2,1)}, bf16[2,192,256]{2,1,0:T(8,128)(2,1)S(1)}, u32[]{:S(2)}) copy-start(bf16[2,192,256]{2,1,0:T(8,128)(2,1)S(1)} %collective-permute-done.4.refs_4_) | copy-start | bytes 589828
  58.2 6.8 %collective-permute-start.6 = (bf16[2,192,256]{2,1,0:T(8,128)(2,1)S(1)}, bf16[2,192,256]{2,1,0:T(8,128)(2,1)S(1)}, u32[]{:S(2)}, u32[]{:S(2)}) collective-permute-start(bf16[2,192,256]{2,1,0:T(8,128)(2,1)S(1)} %collective-permute-done.4.refs_4_), channel_id=1, source_target_pairs={{0,224},{32,0},{64,32},{96,64},{128,96},{160,128},{192,160},{224,1... | collective-permute-start | bytes 589832 | tf_op jit(solution)/shard_map/ppermute | solution.py:293
  60.2 4.8 %collective-permute-start.9 = (bf16[2,192,256]{2,1,0:T(8,128)(2,1)S(1)}, bf16[2,192,256]{2,1,0:T(8,128)(2,1)S(1)}, u32[]{:S(2)}, u32[]{:S(2)}) collective-permute-start(bf16[2,192,256]{2,1,0:T(8,128)(2,1)S(1)} %pad_maximum_fusion.refs_0_), channel_id=1, source_target_pairs={{0,8},{8,0},{1,9},{9,1},{2,10},{10,2},{3,11},{11,3},{4,12},{12,4},... | collective-permute-start | bytes 589832 | tf_op jit(solution)/shard_map/ppermute | solution.py:297
  60.2 8.4 %collective-permute-start.10 = (bf16[2,192,256]{2,1,0:T(8,128)(2,1)S(1)}, bf16[2,192,256]{2,1,0:T(8,128)(2,1)S(1)}, u32[]{:S(2)}, u32[]{:S(2)}) collective-permute-start(bf16[2,192,256]{2,1,0:T(8,128)(2,1)S(1)} %collective-permute-done.1.refs_1_), channel_id=1, source_target_pairs={{0,8},{8,0},{1,9},{9,1},{2,10},{10,2},{3,11},{11,3},{4,12},{12,4},... | collective-permute-start | bytes 589832 | tf_op jit(solution)/shard_map/ppermute | solution.py:297
  60.7 8.0 %collective-permute-start.11 = (bf16[2,192,256]{2,1,0:T(8,128)(2,1)S(1)}, bf16[2,192,256]{2,1,0:T(8,128)(2,1)S(1)}, u32[]{:S(2)}, u32[]{:S(2)}) collective-permute-start(bf16[2,192,256]{2,1,0:T(8,128)(2,1)S(1)} %collective-permute-done.2.refs_2_), channel_id=1, source_target_pairs={{0,8},{8,0},{1,9},{9,1},{2,10},{10,2},{3,11},{11,3},{4,12},{12,4},... | collective-permute-start | bytes 589832 | tf_op jit(solution)/shard_map/ppermute | solution.py:297
  63.7 14.0 %copy-start.6 = (bf16[2,192,256]{2,1,0:T(8,128)(2,1)}, bf16[2,192,256]{2,1,0:T(8,128)(2,1)S(1)}, u32[]{:S(2)}) copy-start(bf16[2,192,256]{2,1,0:T(8,128)(2,1)S(1)} %collective-permute-done.5.refs_5_) | copy-start | bytes 589828
  63.7 5.2 %collective-permute-start.12 = (bf16[2,192,256]{2,1,0:T(8,128)(2,1)S(1)}, bf16[2,192,256]{2,1,0:T(8,128)(2,1)S(1)}, u32[]{:S(2)}, u32[]{:S(2)}) collective-permute-start(bf16[2,192,256]{2,1,0:T(8,128)(2,1)S(1)} %collective-permute-done.3.refs_3_), channel_id=1, source_target_pairs={{0,8},{8,0},{1,9},{9,1},{2,10},{10,2},{3,11},{11,3},{4,12},{12,4},... | collective-permute-start | bytes 589832 | tf_op jit(solution)/shard_map/ppermute | solution.py:297
  65.0 12.7 %copy-start.7 = (bf16[2,192,256]{2,1,0:T(8,128)(2,1)}, bf16[2,192,256]{2,1,0:T(8,128)(2,1)S(1)}, u32[]{:S(2)}) copy-start(bf16[2,192,256]{2,1,0:T(8,128)(2,1)S(1)} %collective-permute-done.6.refs_6_) | copy-start | bytes 589828
  65.0 10.1 %collective-permute-start.13 = (bf16[2,192,256]{2,1,0:T(8,128)(2,1)S(1)}, bf16[2,192,256]{2,1,0:T(8,128)(2,1)S(1)}, u32[]{:S(2)}, u32[]{:S(2)}) collective-permute-start(bf16[2,192,256]{2,1,0:T(8,128)(2,1)S(1)} %collective-permute-done.4.refs_4_), channel_id=1, source_target_pairs={{0,8},{8,0},{1,9},{9,1},{2,10},{10,2},{3,11},{11,3},{4,12},{12,4},... | collective-permute-start | bytes 589832 | tf_op jit(solution)/shard_map/ppermute | solution.py:297
  65.0 12.7 %copy-start.18 = (bf16[2,192,256]{2,1,0:T(8,128)(2,1)}, bf16[2,192,256]{2,1,0:T(8,128)(2,1)S(1)}, u32[]{:S(2)}) copy-start(bf16[2,192,256]{2,1,0:T(8,128)(2,1)S(1)} %collective-permute-done.9.refs_9_) | copy-start | bytes 589828
  65.0 6.3 %collective-permute-start.7 = (bf16[1,192,256]{2,1,0:T(8,128)(2,1)S(1)}, bf16[1,192,256]{2,1,0:T(8,128)(2,1)S(1)}, u32[]{:S(2)}, u32[]{:S(2)}) collective-permute-start(bf16[1,192,256]{2,1,0:T(8,128)(2,1)S(1)} %slice.37), channel_id=1, source_target_pairs={{0,32},{32,64},{64,96},{96,128},{128,160},{160,192},{192,224},{224... | collective-permute-start | bytes 294920 | tf_op jit(solution)/shard_map/ppermute | solution.py:295
  68.6 9.1 %copy-start.19 = (bf16[2,192,256]{2,1,0:T(8,128)(2,1)}, bf16[2,192,256]{2,1,0:T(8,128)(2,1)S(1)}, u32[]{:S(2)}) copy-start(bf16[2,192,256]{2,1,0:T(8,128)(2,1)S(1)} %collective-permute-done.10.refs_10_) | copy-start | bytes 589828
  68.6 6.4 %collective-permute-start.8 = (bf16[1,192,256]{2,1,0:T(8,128)(2,1)S(1)}, bf16[1,192,256]{2,1,0:T(8,128)(2,1)S(1)}, u32[]{:S(2)}, u32[]{:S(2)}) collective-permute-start(bf16[1,192,256]{2,1,0:T(8,128)(2,1)S(1)} %slice.38), channel_id=1, source_target_pairs={{0,224},{32,0},{64,32},{96,64},{128,96},{160,128},{192,160},{224,1... | collective-permute-start | bytes 294920 | tf_op jit(solution)/shard_map/ppermute | solution.py:296
  68.7 9.1 %copy-start.20 = (bf16[2,192,256]{2,1,0:T(8,128)(2,1)}, bf16[2,192,256]{2,1,0:T(8,128)(2,1)S(1)}, u32[]{:S(2)}) copy-start(bf16[2,192,256]{2,1,0:T(8,128)(2,1)S(1)} %collective-permute-done.11.refs_11_) | copy-start | bytes 589828
  68.7 7.7 %collective-permute-start.14 = (bf16[2,192,256]{2,1,0:T(8,128)(2,1)S(1)}, bf16[2,192,256]{2,1,0:T(8,128)(2,1)S(1)}, u32[]{:S(2)}, u32[]{:S(2)}) collective-permute-start(bf16[2,192,256]{2,1,0:T(8,128)(2,1)S(1)} %collective-permute-done.5.refs_5_), channel_id=1, source_target_pairs={{0,8},{8,0},{1,9},{9,1},{2,10},{10,2},{3,11},{11,3},{4,12},{12,4},... | collective-permute-start | bytes 589832 | tf_op jit(solution)/shard_map/ppermute | solution.py:297
  69.0 8.8 %copy-start.21 = (bf16[2,192,256]{2,1,0:T(8,128)(2,1)}, bf16[2,192,256]{2,1,0:T(8,128)(2,1)S(1)}, u32[]{:S(2)}) copy-start(bf16[2,192,256]{2,1,0:T(8,128)(2,1)S(1)} %collective-permute-done.12.refs_12_) | copy-start | bytes 589828
  69.0 8.7 %collective-permute-start.15 = (bf16[2,192,256]{2,1,0:T(8,128)(2,1)S(1)}, bf16[2,192,256]{2,1,0:T(8,128)(2,1)}, u32[]{:S(2)}, u32[]{:S(2)}) collective-permute-start(bf16[2,192,256]{2,1,0:T(8,128)(2,1)S(1)} %collective-permute-done.6.refs_6_), channel_id=1, source_target_pairs={{0,8},{8,0},{1,9},{9,1},{2,10},{10,2},{3,11},{11,3},{4,12},{12,4},... | collective-permute-start | bytes 589832 | tf_op jit(solution)/shard_map/ppermute | solution.py:297
  71.3 5.0 %copy-start.24 = (bf16[1,192,256]{2,1,0:T(8,128)(2,1)}, bf16[1,192,256]{2,1,0:T(8,128)(2,1)S(1)}, u32[]{:S(2)}) copy-start(bf16[1,192,256]{2,1,0:T(8,128)(2,1)S(1)} %collective-permute-done.7.refs_7_) | copy-start | bytes 294916
  71.3 3.7 %collective-permute-start.16 = (bf16[1,192,256]{2,1,0:T(8,128)(2,1)S(1)}, bf16[1,192,256]{2,1,0:T(8,128)(2,1)S(1)}, u32[]{:S(2)}, u32[]{:S(2)}) collective-permute-start(bf16[1,192,256]{2,1,0:T(8,128)(2,1)S(1)} %collective-permute-done.7.refs_7_), channel_id=1, source_target_pairs={{0,8},{8,0},{1,9},{9,1},{2,10},{10,2},{3,11},{11,3},{4,12},{12,4},... | collective-permute-start | bytes 294920 | tf_op jit(solution)/shard_map/ppermute | solution.py:297
  75.0 1.3 collective-permute-start.17
  90.8 33.1 %copy-start.11 = (bf16[8,96,256]{2,1,0:T(8,128)(2,1)S(1)}, bf16[8,96,256]{2,1,0:T(8,128)(2,1)}, u32[]{:S(2)}) copy-start(bf16[8,96,256]{2,1,0:T(8,128)(2,1)} %get-tuple-element.41) | copy-start | bytes 1179652
  90.9 5.4 %collective-permute-start.22 = (bf16[8,96,256]{2,1,0:T(8,128)(2,1)}, bf16[8,96,256]{2,1,0:T(8,128)(2,1)S(1)}, u32[]{:S(2)}, u32[]{:S(2)}) collective-permute-start(bf16[8,96,256]{2,1,0:T(8,128)(2,1)} %get-tuple-element.46), channel_id=1, source_target_pairs={{0,8},{8,0},{1,9},{9,1},{2,10},{10,2},{3,11},{11,3},{4,12},{12,4},... | collective-permute-start | bytes 1179656 | tf_op jit(solution)/shard_map/ppermute | solution.py:314
  94.7 6.5 %collective-permute-start.21 = (bf16[8,96,256]{2,1,0:T(8,128)(2,1)}, bf16[8,96,256]{2,1,0:T(8,128)(2,1)S(1)}, u32[]{:S(2)}, u32[]{:S(2)}) collective-permute-start(bf16[8,96,256]{2,1,0:T(8,128)(2,1)} %get-tuple-element.44), channel_id=1, source_target_pairs={{0,8},{8,0},{1,9},{9,1},{2,10},{10,2},{3,11},{11,3},{4,12},{12,4},... | collective-permute-start | bytes 1179656 | tf_op jit(solution)/shard_map/ppermute | solution.py:315
  97.4 36.8 %copy-start.10 = (bf16[8,96,256]{2,1,0:T(8,128)(2,1)S(1)}, bf16[8,96,256]{2,1,0:T(8,128)(2,1)}, u32[]{:S(2)}) copy-start(bf16[8,96,256]{2,1,0:T(8,128)(2,1)} %get-tuple-element.39) | copy-start | bytes 1179652
  97.4 12.7 %collective-permute-start.23 = (bf16[8,96,256]{2,1,0:T(8,128)(2,1)S(1)}, bf16[8,96,256]{2,1,0:T(8,128)(2,1)S(1)}, u32[]{:S(2)}, u32[]{:S(2)}) collective-permute-start(bf16[8,96,256]{2,1,0:T(8,128)(2,1)S(1)} %add_convert_fusion.1), channel_id=1, source_target_pairs={{0,16},{16,0},{1,17},{17,1},{2,18},{18,2},{3,19},{19,3},{4,20},{20... | collective-permute-start | bytes 1179656 | tf_op jit(solution)/shard_map/ppermute | solution.py:316
  100.7 23.3 %collective-permute-start.19 = (bf16[8,96,256]{2,1,0:T(8,128)(2,1)}, bf16[8,96,256]{2,1,0:T(8,128)(2,1)S(1)}, u32[]{:S(2)}, u32[]{:S(2)}) collective-permute-start(bf16[8,96,256]{2,1,0:T(8,128)(2,1)} %get-tuple-element.42), channel_id=1, source_target_pairs={{0,8},{8,0},{1,9},{9,1},{2,10},{10,2},{3,11},{11,3},{4,12},{12,4},... | collective-permute-start | bytes 1179656 | tf_op jit(solution)/shard_map/ppermute | solution.py:314
  100.7 23.8 %collective-permute-start.18 = (bf16[8,96,256]{2,1,0:T(8,128)(2,1)}, bf16[8,96,256]{2,1,0:T(8,128)(2,1)S(1)}, u32[]{:S(2)}, u32[]{:S(2)}) collective-permute-start(bf16[8,96,256]{2,1,0:T(8,128)(2,1)} %get-tuple-element.40), channel_id=1, source_target_pairs={{0,8},{8,0},{1,9},{9,1},{2,10},{10,2},{3,11},{11,3},{4,12},{12,4},... | collective-permute-start | bytes 1179656 | tf_op jit(solution)/shard_map/ppermute | solution.py:315
  112.0 24.9 %all-to-all-start.2 = ((bf16[8,96,256]{2,1,0:T(8,128)(2,1)}), bf16[8,96,256]{2,1,0:T(8,128)(2,1)S(1)}, u32[]{:S(2)}, u32[]{:S(2)}) async-start(bf16[8,96,256]{2,1,0:T(8,128)(2,1)} %add_convert_fusion), calls=%async_computation.2 | async-start | bytes 786432 | tf_op jit(solution)/shard_map/all_to_all | solution.py:318
  124.1 10.1 %collective-permute-start.20 = (bf16[8,96,256]{2,1,0:T(8,128)(2,1)S(1)}, bf16[8,96,256]{2,1,0:T(8,128)(2,1)S(1)}, u32[]{:S(2)}, u32[]{:S(2)}) collective-permute-start(bf16[8,96,256]{2,1,0:T(8,128)(2,1)S(1)} %add_convert_fusion.3), channel_id=1, source_target_pairs={{0,16},{16,0},{1,17},{17,1},{2,18},{18,2},{3,19},{19,3},{4,20},{20... | collective-permute-start | bytes 1179656 | tf_op jit(solution)/shard_map/ppermute | solution.py:316
  136.9 16.9 %all-to-all-start.1 = ((bf16[8,96,256]{2,1,0:T(8,128)(2,1)}), bf16[8,96,256]{2,1,0:T(8,128)(2,1)S(1)}, u32[]{:S(2)}, u32[]{:S(2)}) async-start(bf16[8,96,256]{2,1,0:T(8,128)(2,1)} %add_convert_fusion.2), calls=%async_computation.1 | async-start | bytes 786432 | tf_op jit(solution)/shard_map/all_to_all | solution.py:318
  146.9 18.5 %collective-permute-start.25 = (bf16[16,160,192]{2,1,0:T(8,128)(2,1)}, bf16[16,160,192]{2,1,0:T(8,128)(2,1)}, u32[]{:S(2)}, u32[]{:S(2)}) collective-permute-start(bf16[16,160,192]{2,1,0:T(8,128)(2,1)} %get-tuple-element.50), channel_id=1, source_target_pairs={{0,8},{8,0},{1,9},{9,1},{2,10},{10,2},{3,11},{11,3},{4,12},{12,4},... | collective-permute-start | bytes 2949128 | tf_op jit(solution)/shard_map/ppermute | solution.py:301
  154.5 1.9 copy-start.2
  154.5 4.6 %collective-permute-start.24 = (bf16[192,256]{1,0:T(8,128)(2,1)S(1)}, bf16[192,256]{1,0:T(8,128)(2,1)S(1)}, u32[]{:S(2)}, u32[]{:S(2)}) collective-permute-start(bf16[192,256]{1,0:T(8,128)(2,1)S(1)} %get-tuple-element.66.own_ref), channel_id=1, source_target_pairs={{0,16},{16,0},{1,17},{17,1},{2,18},{18,2},{3,19},{19,3},{4,20},{20... | collective-permute-start | bytes 294920 | tf_op jit(solution)/shard_map/ppermute | solution.py:322
  159.1 9.4 %copy-start.9 = (bf16[192,256]{1,0:T(8,128)(2,1)}, bf16[192,256]{1,0:T(8,128)(2,1)S(1)}, u32[]{:S(2)}) copy-start(bf16[192,256]{1,0:T(8,128)(2,1)S(1)} %collective-permute-done.24.side_ref) | copy-start | bytes 294916
  159.1 78.8 %all-to-all-start.3 = ((bf16[8,24,5120]{2,1,0:T(8,128)(2,1)}), bf16[8,24,5120]{2,1,0:T(8,128)(2,1)S(1)}, u32[]{:S(2)}, u32[]{:S(2)}) async-start(bf16[8,24,5120]{2,1,0:T(8,128)(2,1)} %bitcast.7), calls=%async_computation.3 | async-start | bytes 3932160 | tf_op jit(solution)/shard_map/all_to_all | solution.py:330
  164.1 4.3 %copy-start.12 = (bf16[1,192,256]{2,1,0:T(8,128)(2,1)S(1)}, bf16[1,192,256]{2,1,0:T(8,128)(2,1)}, u32[]{:S(2)}) copy-start(bf16[1,192,256]{2,1,0:T(8,128)(2,1)} %get-tuple-element.65) | copy-start | bytes 294916
  164.1 38.0 %collective-permute-start.26 = (bf16[8,160,192]{2,1,0:T(8,128)(2,1)}, bf16[8,160,192]{2,1,0:T(8,128)(2,1)S(1)}, u32[]{:S(2)}, u32[]{:S(2)}) collective-permute-start(bf16[8,160,192]{2,1,0:T(8,128)(2,1)} %get-tuple-element.51), channel_id=1, source_target_pairs={{0,16},{16,0},{1,17},{17,1},{2,18},{18,2},{3,19},{19,3},{4,20},{20... | collective-permute-start | bytes 1474568 | tf_op jit(solution)/shard_map/ppermute | solution.py:302
  167.6 42.9 %collective-permute-start.27 = (bf16[8,160,192]{2,1,0:T(8,128)(2,1)S(1)}, bf16[8,160,192]{2,1,0:T(8,128)(2,1)S(1)}, u32[]{:S(2)}, u32[]{:S(2)}) collective-permute-start(bf16[8,160,192]{2,1,0:T(8,128)(2,1)S(1)} %get-tuple-element.61), channel_id=1, source_target_pairs={{0,16},{16,0},{1,17},{17,1},{2,18},{18,2},{3,19},{19,3},{4,20},{20... | collective-permute-start | bytes 1474568 | tf_op jit(solution)/shard_map/ppermute | solution.py:303
  168.5 42.0 %collective-permute-start.28 = (bf16[2,192,256]{2,1,0:T(8,128)(2,1)S(1)}, bf16[2,192,256]{2,1,0:T(8,128)(2,1)S(1)}, u32[]{:S(2)}, u32[]{:S(2)}) collective-permute-start(bf16[2,192,256]{2,1,0:T(8,128)(2,1)S(1)} %pad_maximum_fusion.1), channel_id=1, source_target_pairs={{0,8},{8,0},{1,9},{9,1},{2,10},{10,2},{3,11},{11,3},{4,12},{12,4},... | collective-permute-start | bytes 589832 | tf_op jit(solution)/shard_map/ppermute | solution.py:333
  202.1 8.3 %copy-start.4 = (bf16[8,160,192]{2,1,0:T(8,128)(2,1)}, bf16[8,160,192]{2,1,0:T(8,128)(2,1)S(1)}, u32[]{:S(2)}) copy-start(bf16[8,160,192]{2,1,0:T(8,128)(2,1)S(1)} %collective-permute-done.26.c_ref) | copy-start | bytes 1474564
  215.3 12.3 %collective-permute-start.29 = (bf16[160,256]{1,0:T(8,128)(2,1)}, bf16[160,256]{1,0:T(8,128)(2,1)S(1)}, u32[]{:S(2)}, u32[]{:S(2)}) collective-permute-start(bf16[160,256]{1,0:T(8,128)(2,1)} %get-tuple-element.54), channel_id=1, source_target_pairs={{0,32},{32,64},{64,96},{96,128},{128,160},{160,192},{192,224},{224... | collective-permute-start | bytes 245768 | tf_op jit(solution)/shard_map/ppermute | solution.py:337
  217.0 11.6 %collective-permute-start.30 = (bf16[160,256]{1,0:T(8,128)(2,1)}, bf16[160,256]{1,0:T(8,128)(2,1)S(1)}, u32[]{:S(2)}, u32[]{:S(2)}) collective-permute-start(bf16[160,256]{1,0:T(8,128)(2,1)} %get-tuple-element.55), channel_id=1, source_target_pairs={{0,64},{32,96},{64,128},{96,160},{128,192},{160,224},{192,0},{224,... | collective-permute-start | bytes 245768 | tf_op jit(solution)/shard_map/ppermute | solution.py:337
  218.4 12.3 %collective-permute-start.31 = (bf16[160,256]{1,0:T(8,128)(2,1)}, bf16[160,256]{1,0:T(8,128)(2,1)S(1)}, u32[]{:S(2)}, u32[]{:S(2)}) collective-permute-start(bf16[160,256]{1,0:T(8,128)(2,1)} %get-tuple-element.56), channel_id=1, source_target_pairs={{0,96},{32,128},{64,160},{96,192},{128,224},{160,0},{192,32},{224,... | collective-permute-start | bytes 245768 | tf_op jit(solution)/shard_map/ppermute | solution.py:337
  220.7 10.9 %collective-permute-start.32 = (bf16[160,256]{1,0:T(8,128)(2,1)}, bf16[160,256]{1,0:T(8,128)(2,1)S(1)}, u32[]{:S(2)}, u32[]{:S(2)}) collective-permute-start(bf16[160,256]{1,0:T(8,128)(2,1)} %get-tuple-element.57), channel_id=1, source_target_pairs={{0,128},{32,160},{64,192},{96,224},{128,0},{160,32},{192,64},{224,... | collective-permute-start | bytes 245768 | tf_op jit(solution)/shard_map/ppermute | solution.py:337
  223.9 11.8 %collective-permute-start.33 = (bf16[160,256]{1,0:T(8,128)(2,1)}, bf16[160,256]{1,0:T(8,128)(2,1)S(1)}, u32[]{:S(2)}, u32[]{:S(2)}) collective-permute-start(bf16[160,256]{1,0:T(8,128)(2,1)} %get-tuple-element.58), channel_id=1, source_target_pairs={{0,160},{32,192},{64,224},{96,0},{128,32},{160,64},{192,96},{224,1... | collective-permute-start | bytes 245768 | tf_op jit(solution)/shard_map/ppermute | solution.py:337
  227.6 8.1 %collective-permute-start.34 = (bf16[160,256]{1,0:T(8,128)(2,1)}, bf16[160,256]{1,0:T(8,128)(2,1)S(1)}, u32[]{:S(2)}, u32[]{:S(2)}) collective-permute-start(bf16[160,256]{1,0:T(8,128)(2,1)} %get-tuple-element.59), channel_id=1, source_target_pairs={{0,192},{32,224},{64,0},{96,32},{128,64},{160,96},{192,128},{224,1... | collective-permute-start | bytes 245768 | tf_op jit(solution)/shard_map/ppermute | solution.py:337
  228.6 7.6 %collective-permute-start.35 = (bf16[160,256]{1,0:T(8,128)(2,1)}, bf16[160,256]{1,0:T(8,128)(2,1)S(1)}, u32[]{:S(2)}, u32[]{:S(2)}) collective-permute-start(bf16[160,256]{1,0:T(8,128)(2,1)} %get-tuple-element.60), channel_id=1, source_target_pairs={{0,224},{32,0},{64,32},{96,64},{128,96},{160,128},{192,160},{224,1... | collective-permute-start | bytes 245768 | tf_op jit(solution)/shard_map/ppermute | solution.py:337
  (8 other events, 8.7 us)
